TPU v7x, 32 devices: a whole 2x2x4 slice. The times are simulated.
32 devices in a mesh: inner: 8 (over y, x, core), outer: 4 (over z).
Axes of the slice: x: 2, y: 2, z: 4, core: 2. Of those that a mesh axis runs over, the one named last changes fastest.
Arguments:
- hidden: bfloat16 [8192, 1152], P(('inner', 'outer')), may hold values from -6 to 6
- latents_now: float32 [32, 16, 256], P(('inner', 'outer')), may hold values from -6 to 6
- latents_next: float32 [32, 16, 256], P(('inner', 'outer')), may hold values from -6.3 to 6.3
- timestep: int32 [1], replicated, may hold values from 3 to 9
- version_tags: int32 [32], P(('inner', 'outer')), may hold values from 0 to 7
- noise_levels: float32 [8], replicated, may hold values from 0.5 to 1
- time_weight: bfloat16 [256, 6912], replicated, may hold values from -0.375 to 0.375
- spatial_qkv: bfloat16 [1152, 3456], replicated, may hold values from -0.1875 to 0.1875
- spatial_out: bfloat16 [1152, 1152], replicated, may hold values from -0.1875 to 0.1875
- temporal_qkv: bfloat16 [1152, 3456], replicated, may hold values from -0.1875 to 0.1875
- temporal_out: bfloat16 [1152, 1152], replicated, may hold values from -0.1875 to 0.1875
- final_weight: bfloat16 [16, 1152], replicated, may hold values from -0.1875 to 0.1875
Outputs:
- log_prob: float32 [32, 256], P(('inner', 'outer'))
- next_mean: float32 [32, 16, 256], P(('inner', 'outer'))
Inputs may be any that keep to these rules, and one draw needn't show every extreme that they name: `timestep`: the index k of the denoising step, whose time is k / 10.
All inputs are finite; a program needn't handle non-finite values.
Results may differ from a plain program's by a relative error of at most 0.004.
Values may be sent and summed in bfloat16 or wider, within the bound.
A program may use at most 128 MiB of HBM per device.

v0:
```python
import functools
import math

import jax
import jax.numpy as jnp
from jax import lax
from jax.experimental import pallas as pl
from jax.experimental.pallas import tpu as pltpu
from jax.sharding import PartitionSpec as P

HEADS = 16
STEPS = 10
LANES = 128
WINDOW = 256
GROUP = 8
norm_eps = 1e-06
f32 = jnp.float32
bf16 = jnp.bfloat16
MESH = pl.DeviceIdType.MESH


def layer_norm(values):
    average = jnp.mean(values, -1, keepdims=True)
    centred = values - average
    variance = jnp.mean(centred * centred, -1, keepdims=True)
    return centred * lax.rsqrt(variance + norm_eps)


def split_pair(values):
    high = values.astype(bf16)
    return high, (values - high.astype(f32)).astype(bf16)


def dot(a, b):
    return jnp.dot(a, b, preferred_element_type=f32)


def dot_t(a, b):
    return lax.dot_general(a, b, (((1,), (1,)), ((), ())), preferred_element_type=f32)


def kernel(
    sizes,
    hidden_hbm,
    now_hbm,
    next_hbm,
    step_ref,
    tag_ref,
    level_ref,
    final_hbm,
    time_hbm,
    sqkv_hbm,
    sout_hbm,
    tqkv_hbm,
    tout_hbm,
    logp_ref,
    mean_ref,
    hidden_ref,
    now_ref,
    next_ref,
    final_ref,
    time_w,
    sqkv_w,
    sout_w,
    tqkv_w,
    tout_w,
    table,
    group_ref,
    spread_ref,
    mask_ref,
    q_ref,
    k_ref,
    v_ref,
    after_ref,
    out_buf,
    in_buf,
    back_buf,
    ret_buf,
    w_sem,
    send_sem,
    recv_sem,
    send2_sem,
    recv2_sem,
):
    inner_size, outer_size = sizes
    peers = inner_size * outer_size
    rows, width = hidden_hbm.shape
    count = rows // peers
    head = width // HEADS
    half_peers = peers // 2
    half_rows = rows // 2
    chips = inner_size // 2
    inner = lax.axis_index("inner")
    outer = lax.axis_index("outer")
    core = lax.rem(inner, 2)
    chip = inner // 2
    me = inner * outer_size + outer

    my_block = core * half_peers + chip * outer_size + outer

    far = outer_size // 2 if outer_size % 2 == 0 else 0

    def outer_of(j):
        span = outer_size - far
        side = outer // span
        crossing = (1 - side) * far + lax.rem(outer + j, span)
        same = side * span + lax.rem(outer + j - far, span)
        return jnp.where(j < far, crossing, same)

    def fetch(source, target, index, lo, hi):
        return pltpu.make_async_copy(
            source.at[:, lo:hi], target.at[:, lo:hi], w_sem.at[index]
        )

    loads = [
        fetch(time_hbm, time_w, 0, 0, 2 * width),
        fetch(sqkv_hbm, sqkv_w, 1, 0, width),
        fetch(sqkv_hbm, sqkv_w, 2, width, 2 * width),
        fetch(sqkv_hbm, sqkv_w, 3, 2 * width, 3 * width),
        fetch(time_hbm, time_w, 4, 2 * width, 6 * width),
        fetch(sout_hbm, sout_w, 5, 0, width),
        fetch(tqkv_hbm, tqkv_w, 6, 0, 3 * width),
        fetch(tout_hbm, tout_w, 7, 0, width),
    ]
    rest = [
        pltpu.make_async_copy(now_hbm, now_ref, w_sem.at[9]),
        pltpu.make_async_copy(next_hbm, next_ref, w_sem.at[10]),
        pltpu.make_async_copy(final_hbm, final_ref, w_sem.at[11]),
    ]
    hidden_load = pltpu.make_async_copy(hidden_hbm, hidden_ref, w_sem.at[8])
    loads[0].start()
    hidden_load.start()
    for load in loads[1:4]:
        load.start()

    barrier = pltpu.get_barrier_semaphore()

    @pl.loop(1, peers)
    def _(k):
        peer = lax.rem(me + k, peers)
        pl.semaphore_signal(
            barrier,
            inc=1,
            device_id=(peer // outer_size, lax.rem(peer, outer_size)),
            device_id_type=MESH,
        )

    feature = lax.broadcasted_iota(jnp.int32, (width, LANES), 0)
    column = lax.broadcasted_iota(jnp.int32, (width, LANES), 1) * head
    group_ref[...] = jnp.where(
        (feature >= column) & (feature < column + head), 1.0, 0.0
    ).astype(bf16)
    feature = lax.broadcasted_iota(jnp.int32, (LANES, width), 1)
    column = lax.broadcasted_iota(jnp.int32, (LANES, width), 0) * head
    spread = jnp.where((feature >= column) & (feature < column + head), 1.0, 0.0).astype(bf16)
    spread_ref[0:LANES, :] = spread
    spread_ref[LANES:, :] = spread

    time_value = jnp.full((8, LANES), step_ref[0].astype(f32)) / STEPS
    lane = lax.broadcasted_iota(jnp.int32, (8, LANES), 1).astype(f32)
    angles = 1000.0 * time_value * jnp.exp(-math.log(10000.0) * lane / LANES)
    embedded = jnp.concatenate([jnp.cos(angles), jnp.sin(angles)], 1)
    activated = (embedded / (1.0 + jnp.exp(-embedded))).astype(bf16)
    loads[0].wait()
    loads[5].start()
    loads[4].start()
    table[:, 0 : 2 * width] = dot(activated, time_w[:, 0 : 2 * width])

    def entry(index):
        return table[0:1, index * width : (index + 1) * width]

    hidden_load.wait()
    hidden = hidden_ref[...].astype(f32)
    normed = (layer_norm(hidden) * (1.0 + entry(1)) + entry(0)).astype(bf16)

    def head_norm(values, factor):
        high, low = split_pair(values * values)
        total = dot(high, group_ref[...]) + dot(low, group_ref[...])
        inverse = lax.rsqrt(total / head + norm_eps) * factor
        high, low = split_pair(inverse)
        return (values * dot(jnp.concatenate([high, low], 1), spread_ref[...])).astype(bf16)

    def project(normed, weight, waits):
        waits[0]()
        q_ref[...] = head_norm(dot(normed, weight[:, 0:width]), head**-0.5)
        waits[1]()
        k_ref[...] = head_norm(dot(normed, weight[:, width : 2 * width]), 1.0)
        waits[2]()
        v_ref[...] = dot(normed, weight[:, 2 * width : 3 * width]).astype(bf16)

    def attend(lo, size, masked):
        tiles = width // LANES
        tops, bottoms = [None] * tiles, [None] * tiles
        lane = lax.broadcasted_iota(jnp.int32, (1, WINDOW), 1)

        def window_of(index):
            tile = min(index * head // LANES, (width - WINDOW) // LANES)
            inside = (lane >= index * head - tile * LANES) & (
                lane < (index + 1) * head - tile * LANES
            )
            return tile, jnp.where(inside, 1.0, 0.0).astype(bf16)

        for first in range(0, HEADS, GROUP):
            group = range(first, first + GROUP)
            scores = []
            for index in group:
                tile, own = window_of(index)
                window = slice(tile * LANES, tile * LANES + WINDOW)
                scores.append(dot_t(q_ref[lo : lo + size, window] * own, k_ref[:, window]))
            weights = []
            for score in scores:
                weight = jnp.exp(score).astype(bf16)
                if masked:
                    weight = weight * mask_ref[lo : lo + size, :]
                weights.append(weight)
            for index, weight in zip(group, weights):
                tile, own = window_of(index)
                window = slice(tile * LANES, tile * LANES + WINDOW)
                mixed = dot(weight, v_ref[:, window] * own + (1.0 - own))
                for side in range(WINDOW // LANES):
                    begin = index * head - (tile + side) * LANES
                    if begin >= LANES or begin + head <= 0:
                        continue
                    top = mixed[:, side * LANES : (side + 1) * LANES]
                    bottom = mixed[:, (1 - side) * LANES : (2 - side) * LANES]
                    here = tile + side
                    if tops[here] is None:
                        tops[here], bottoms[here] = top, bottom
                    else:
                        short = lane[:, :LANES] >= begin
                        tops[here] = jnp.where(short, top, tops[here])
                        bottoms[here] = jnp.where(short, bottom, bottoms[here])
        return jnp.concatenate(
            [(top / bottom).astype(bf16) for top, bottom in zip(tops, bottoms)], 1
        )

    project(normed, sqkv_w, [loads[1].wait, loads[2].wait, loads[3].wait])
    loads[6].start()
    loads[7].start()
    for load in rest:
        load.start()
    loads[4].wait()
    table[:, 2 * width : 5 * width] = dot(activated, time_w[:, 2 * width : 5 * width])
    loads[5].wait()

    def forward(block, inner_id, outer_id):
        return pltpu.make_async_remote_copy(
            src_ref=out_buf.at[block],
            dst_ref=in_buf.at[me],
            send_sem=send_sem.at[block],
            recv_sem=recv_sem.at[me],
            device_id=(inner_id, outer_id),
            device_id_type=MESH,
        )

    for part in range(2):
        lo = part * half_rows
        attended = attend(lo, half_rows, False)
        projected = dot(attended, sout_w[...])
        after = (hidden_ref[lo : lo + half_rows, :].astype(f32) + entry(2) * projected).astype(bf16)
        after_ref[lo : lo + half_rows, :] = after
        values = layer_norm(after.astype(f32)) * (1.0 + entry(4)) + entry(3)
        out_buf[part * half_peers : (part + 1) * half_peers] = values.reshape(
            half_peers, count, width
        ).astype(bf16)
        if part == 0:
            pl.semaphore_wait(barrier, peers - 1)

        def send(k):
            to_chip = lax.rem(chip + lax.rem(k, chips), chips)
            to_outer = outer_of(k // chips)
            block = part * half_peers + to_chip * outer_size + to_outer
            forward(block, 2 * to_chip + part, to_outer).start()

        own = far * chips

        @pl.loop(0, own)
        def _(k):
            send(k)

        @pl.loop(own + 1, half_peers)
        def _(k):
            send(k)

        @pl.when(core != part)
        def _():
            send(own)

        @pl.when(core == part)
        def _():
            in_buf[me] = out_buf[my_block]

    place = lax.rem(lax.broadcasted_iota(jnp.int32, (rows, rows), 0), count)
    other = lax.rem(lax.broadcasted_iota(jnp.int32, (rows, rows), 1), count)
    mask_ref[...] = jnp.where(place == other, 1.0, 0.0).astype(bf16)
    table[:, 5 * width :] = dot(activated, time_w[:, 5 * width :])
    loads[6].wait()
    loads[7].wait()
    for load in rest:
        load.wait()

    @pl.loop(1, peers)
    def _(k):
        peer = lax.rem(me + k, peers)
        pltpu.make_async_remote_copy(
            src_ref=out_buf.at[0],
            dst_ref=in_buf.at[peer],
            send_sem=send_sem.at[0],
            recv_sem=recv_sem.at[peer],
            device_id=(inner, outer),
            device_id_type=MESH,
        ).wait_recv()

    arrived = in_buf[...].astype(f32).reshape(rows, width).astype(bf16)
    nothing = lambda: None
    project(arrived, tqkv_w, [nothing] * 3)
    attended = attend(0, rows, True)
    back_buf[...] = dot(attended, tout_w[...]).reshape(peers, count, width).astype(bf16)

    def send_back(k):
        to_inner = lax.rem(inner + lax.rem(k, inner_size), inner_size)
        to_outer = outer_of(k // inner_size)
        peer = to_inner * outer_size + to_outer
        pltpu.make_async_remote_copy(
            src_ref=back_buf.at[peer],
            dst_ref=ret_buf.at[my_block],
            send_sem=send2_sem.at[peer],
            recv_sem=recv2_sem.at[my_block],
            device_id=(to_inner, to_outer),
            device_id_type=MESH,
        ).start()

    own = far * inner_size

    @pl.loop(0, own)
    def _(k):
        send_back(k)

    @pl.loop(own + 1, peers)
    def _(k):
        send_back(k)

    ret_buf[my_block] = back_buf[me]

    @pl.loop(1, peers)
    def _(k):
        block = lax.rem(my_block + k, peers)
        pltpu.make_async_remote_copy(
            src_ref=back_buf.at[0],
            dst_ref=ret_buf.at[block],
            send_sem=send2_sem.at[0],
            recv_sem=recv2_sem.at[block],
            device_id=(inner, outer),
            device_id_type=MESH,
        ).wait_recv()

    term = ret_buf[...].astype(f32).reshape(rows, width)
    state = after_ref[...].astype(f32) + entry(5) * term
    velocity = dot_t(final_ref[...], layer_norm(state).astype(bf16))

    level = jnp.float32(0.0)
    for version in range(level_ref.shape[0]):
        level = level + jnp.where(tag_ref[0] == version, level_ref[version], 0.0)
    time_row = jnp.full((1, rows), step_ref[0].astype(f32)) / STEPS
    noise_scale = level * jnp.sqrt(time_row / (1.0 - time_row))
    factor = noise_scale * noise_scale / (2.0 * time_row)
    now = now_ref[0]
    drift = velocity + factor * (now + (1.0 - time_row) * velocity)
    next_mean = now - drift / STEPS
    mean_ref[0] = next_mean
    deviation = noise_scale * math.sqrt(1.0 / STEPS)
    standard = (next_ref[0] - next_mean) / deviation
    logp_ref[...] = (
        -0.5 * jnp.mean(standard * standard, 0, keepdims=True)
        - jnp.log(deviation)
        - 0.5 * math.log(2.0 * math.pi)
    )

    @pl.loop(1, peers)
    def _(k):
        block = lax.rem(my_block + k, peers)
        peer = lax.rem(me + k, peers)
        pltpu.make_async_remote_copy(
            src_ref=out_buf.at[block],
            dst_ref=in_buf.at[0],
            send_sem=send_sem.at[block],
            recv_sem=recv_sem.at[0],
            device_id=(inner, outer),
            device_id_type=MESH,
        ).wait_send()
        pltpu.make_async_remote_copy(
            src_ref=back_buf.at[peer],
            dst_ref=ret_buf.at[0],
            send_sem=send2_sem.at[peer],
            recv_sem=recv2_sem.at[0],
            device_id=(inner, outer),
            device_id_type=MESH,
        ).wait_send()


def shards(sizes, hidden, now, following, step, tags, levels, time_w, sqkv, sout, tqkv, tout, final):
    peers = sizes[0] * sizes[1]
    rows, width = hidden.shape
    count = rows // peers
    vmem = pl.BlockSpec(memory_space=pltpu.VMEM)
    smem = pl.BlockSpec(memory_space=pltpu.SMEM)
    hbm = pl.BlockSpec(memory_space=pl.ANY)
    exchange = pltpu.VMEM((peers, count, width), bf16)
    sems = pltpu.SemaphoreType.DMA((peers,))
    return pl.pallas_call(
        functools.partial(kernel, sizes),
        out_shape=(pltpu.VMEM((1, rows), f32), pltpu.VMEM(now.shape, f32)),
        in_specs=[hbm, hbm, hbm, smem, smem, smem, hbm] + [hbm] * 5,
        out_specs=(vmem, vmem),
        scratch_shapes=[
            pltpu.VMEM(hidden.shape, bf16),
            pltpu.VMEM(now.shape, f32),
            pltpu.VMEM(following.shape, f32),
            pltpu.VMEM(final.shape, bf16),
            pltpu.VMEM(time_w.shape, bf16),
            pltpu.VMEM(sqkv.shape, bf16),
            pltpu.VMEM(sout.shape, bf16),
            pltpu.VMEM(tqkv.shape, bf16),
            pltpu.VMEM(tout.shape, bf16),
            pltpu.VMEM((8, 6 * width), f32),
            pltpu.VMEM((width, LANES), bf16),
            pltpu.VMEM((2 * LANES, width), bf16),
            pltpu.VMEM((rows, rows), bf16),
            pltpu.VMEM((rows, width), bf16),
            pltpu.VMEM((rows, width), bf16),
            pltpu.VMEM((rows, width), bf16),
            pltpu.VMEM((rows, width), bf16),
            exchange,
            exchange,
            exchange,
            exchange,
            pltpu.SemaphoreType.DMA((12,)),
            sems,
            sems,
            sems,
            sems,
        ],
        compiler_params=pltpu.CompilerParams(
            collective_id=0, has_side_effects=True, vmem_limit_bytes=60 * 1024 * 1024
        ),
    )(hidden, now, following, step, tags, levels, final, time_w, sqkv, sout, tqkv, tout)


def solution(mesh):
    split = P(("inner", "outer"), None)
    split3 = P(("inner", "outer"), None, None)
    sizes = (mesh.shape["inner"], mesh.shape["outer"])
    return jax.shard_map(
        functools.partial(shards, sizes),
        mesh=mesh,
        in_specs=(split, split3, split3, P(), P(("inner", "outer")))
        + (P(),) * 7,
        out_specs=(split, split3),
        check_vma=False,
    )
```

profile of v0, /device:TPU:0, one launch (start us, length us, event | category | flops | bytes accessed | tf_op | source)
XLA Modules:
  0.0 48.7 jit_solution(10974054939050431066)
XLA Ops:
  1.9 45.6 %shard_map.131 = (f32[1,256]{1,0:T(1,128)S(1)}, f32[1,16,256]{2,1,0:T(8,128)S(1)}) custom-call(bf16[256,1152]{1,0:T(8,128)(2,1)} %hidden_hbm.1, f32[1,16,256]{2,1,0:T(8,128)} %now_hbm.1, f32[1,16,256]{2,1,0:T(8,128)} %next_hbm.1, s32[1]{0:T(128)S(6)} %copy.18.step_ref, s32[1]{0:T(128)S(6)} %copy.19.tag_ref, f32[8]{0:T(128)} %level_ref.1, ...), custom_call_target="tpu_custom_call" | custom-call | tf_op jit(solution)/shard_map/pallas_call | solution.py:410
  47.6 0.6 %copy.16 = f32[1,256]{1,0:T(1,128)} copy(f32[1,256]{1,0:T(1,128)S(1)} %get-tuple-element.2) | data formatting | bytes 2048
  48.1 0.6 %copy.17 = f32[1,16,256]{2,1,0:T(8,128)} copy(f32[1,16,256]{2,1,0:T(8,128)S(1)} %get-tuple-element.3) | data formatting | bytes 32768
where the time goes:
time: 48.9 us; the launch traced here: 48.7 us
  Pallas kernels  45.6 us (93%)
  between operations  1.93 us (4%)
  local copies, waits for them, and re-layouts  1.17 us (2%)
    pallas_call x1, Pallas kernels, shards(): pl.pallas_call(functools.partial(kernel, sizes), out_shape=(pltpu.VMEM((1...  45.6 us
    unnamed x2, local copies, waits for them, and re-layouts  1.17 us

commit v1 on v0

--- a/solution.py
+++ b/solution.py
@@ -71,7 +71,6 @@
     q_ref,
     k_ref,
     v_ref,
-    after_ref,
     out_buf,
     in_buf,
     back_buf,
@@ -257,10 +256,8 @@
         lo = part * half_rows
         attended = attend(lo, half_rows, False)
         projected = dot(attended, sout_w[...])
-        after = (hidden_ref[lo : lo + half_rows, :].astype(f32) + entry(2) * projected).astype(bf16)
-        after_ref[lo : lo + half_rows, :] = after
-        values = layer_norm(after.astype(f32)) * (1.0 + entry(4)) + entry(3)
-        out_buf[part * half_peers : (part + 1) * half_peers] = values.reshape(
+        after = hidden_ref[lo : lo + half_rows, :].astype(f32) + entry(2) * projected
+        out_buf[part * half_peers : (part + 1) * half_peers] = after.reshape(
             half_peers, count, width
         ).astype(bf16)
         if part == 0:
@@ -311,11 +308,21 @@
             device_id_type=MESH,
         ).wait_recv()
 
-    arrived = in_buf[...].astype(f32).reshape(rows, width).astype(bf16)
+    after = in_buf[...].astype(f32).reshape(rows, width)
+    normed = (layer_norm(after) * (1.0 + entry(4)) + entry(3)).astype(bf16)
     nothing = lambda: None
-    project(arrived, tqkv_w, [nothing] * 3)
+    project(normed, tqkv_w, [nothing] * 3)
     attended = attend(0, rows, True)
-    back_buf[...] = dot(attended, tout_w[...]).reshape(peers, count, width).astype(bf16)
+    term = dot(attended, tout_w[...]).astype(bf16).astype(f32)
+    after = in_buf[...].astype(f32).reshape(rows, width)
+    final_normed = layer_norm(after + entry(5) * term).astype(bf16)
+    channels = final_ref.shape[0]
+    repeated = jnp.concatenate([final_ref[...]] * (LANES // channels), 0)
+    mixed = dot_t(final_normed, repeated)
+    slot = lax.rem(lax.broadcasted_iota(jnp.int32, (rows, LANES), 0), count)
+    own_slot = slot == lax.broadcasted_iota(jnp.int32, (rows, LANES), 1) // channels
+    packed = jnp.sum(jnp.where(own_slot, mixed, 0.0).reshape(peers, count, LANES), 1)
+    back_buf[...] = packed.reshape(peers, 1, LANES)
 
     def send_back(k):
         to_inner = lax.rem(inner + lax.rem(k, inner_size), inner_size)
@@ -354,9 +361,16 @@
             device_id_type=MESH,
         ).wait_recv()
 
-    term = ret_buf[...].astype(f32).reshape(rows, width)
-    state = after_ref[...].astype(f32) + entry(5) * term
-    velocity = dot_t(final_ref[...], layer_norm(state).astype(bf16))
+    packed = jnp.broadcast_to(ret_buf[...], (peers, count, LANES)).reshape(rows, LANES)
+    packed = jnp.where(own_slot, packed, 0.0)
+    high = packed.astype(bf16)
+    residue = packed - high.astype(f32)
+    middle = residue.astype(bf16)
+    low = (residue - middle.astype(f32)).astype(bf16)
+    lane = lax.broadcasted_iota(jnp.int32, (channels, LANES), 1)
+    pick = lax.rem(lane, channels) == lax.broadcasted_iota(jnp.int32, (channels, LANES), 0)
+    pick = jnp.where(pick, 1.0, 0.0).astype(bf16)
+    velocity = dot_t(pick, high) + dot_t(pick, middle) + dot_t(pick, low)
 
     level = jnp.float32(0.0)
     for version in range(level_ref.shape[0]):
@@ -429,11 +443,10 @@
             pltpu.VMEM((rows, width), bf16),
             pltpu.VMEM((rows, width), bf16),
             pltpu.VMEM((rows, width), bf16),
-            pltpu.VMEM((rows, width), bf16),
             exchange,
             exchange,
-            exchange,
-            exchange,
+            pltpu.VMEM((peers, 1, LANES), f32),
+            pltpu.VMEM((peers, 1, LANES), f32),
             pltpu.SemaphoreType.DMA((12,)),
             sems,
             sems,

time: 48.9 us -> 42.9 us (0.88)
  Pallas kernels: 45.6 us -> 39.6 us
    pallas_call x1, Pallas kernels: 45.6 us -> 39.6 us  [shards(): pl.pallas_call(functools.partial(kernel, sizes), out_shape=(pltpu.VMEM((1...]
where the time goes in v1:
time: 42.9 us; the launch traced here: 42.7 us
  Pallas kernels  39.6 us (92%)
  between operations  1.93 us (4%)
  local copies, waits for them, and re-layouts  1.17 us (3%)
    pallas_call x1, Pallas kernels, shards(): pl.pallas_call(functools.partial(kernel, sizes), out_shape=(pltpu.VMEM((1...  39.6 us
    unnamed x2, local copies, waits for them, and re-layouts  1.17 us

profile of v1, /device:TPU:0, one launch (start us, length us, event | category | flops | bytes accessed | tf_op | source)
XLA Modules:
  0.0 42.7 jit_solution(16353507335359003272)
XLA Ops:
  1.9 39.6 %shard_map.131 = (f32[1,256]{1,0:T(1,128)S(1)}, f32[1,16,256]{2,1,0:T(8,128)S(1)}) custom-call(bf16[256,1152]{1,0:T(8,128)(2,1)} %hidden_hbm.1, f32[1,16,256]{2,1,0:T(8,128)} %now_hbm.1, f32[1,16,256]{2,1,0:T(8,128)} %next_hbm.1, s32[1]{0:T(128)S(6)} %copy.18.step_ref, s32[1]{0:T(128)S(6)} %copy.19.tag_ref, f32[8]{0:T(128)} %level_ref.1, ...), custom_call_target="tpu_custom_call" | custom-call | tf_op jit(solution)/shard_map/pallas_call | solution.py:424
  41.5 0.6 %copy.16 = f32[1,256]{1,0:T(1,128)} copy(f32[1,256]{1,0:T(1,128)S(1)} %get-tuple-element.2) | data formatting | bytes 2048
  42.1 0.6 %copy.17 = f32[1,16,256]{2,1,0:T(8,128)} copy(f32[1,16,256]{2,1,0:T(8,128)S(1)} %get-tuple-element.3) | data formatting | bytes 32768

commit v2 on v0

v2 whole, which is shorter than its diff:
```python
import functools
import math

import jax
import jax.numpy as jnp
from jax import lax
from jax.experimental import pallas as pl
from jax.experimental.pallas import tpu as pltpu
from jax.sharding import PartitionSpec as P

HEADS = 16
STEPS = 10
LANES = 128
WINDOW = 256
GROUP = 8
norm_eps = 1e-06
f32 = jnp.float32
bf16 = jnp.bfloat16
MESH = pl.DeviceIdType.MESH


def layer_norm(values):
    average = jnp.mean(values, -1, keepdims=True)
    centred = values - average
    variance = jnp.mean(centred * centred, -1, keepdims=True)
    return centred * lax.rsqrt(variance + norm_eps)


def split_pair(values):
    high = values.astype(bf16)
    return high, (values - high.astype(f32)).astype(bf16)


def dot(a, b):
    return jnp.dot(a, b, preferred_element_type=f32)


def dot_t(a, b):
    return lax.dot_general(a, b, (((1,), (1,)), ((), ())), preferred_element_type=f32)


def kernel(
    sizes,
    hidden_hbm,
    now_hbm,
    next_hbm,
    step_hbm,
    tag_hbm,
    level_hbm,
    final_hbm,
    time_hbm,
    sqkv_hbm,
    sout_hbm,
    tqkv_hbm,
    tout_hbm,
    logp_ref,
    mean_ref,
    step_ref,
    tag_ref,
    level_ref,
    hidden_ref,
    now_ref,
    next_ref,
    final_ref,
    time_w,
    sqkv_w,
    sout_w,
    tqkv_w,
    tout_w,
    table,
    group_ref,
    spread_ref,
    mask_ref,
    k_ref,
    v_ref,
    out_buf,
    in_buf,
    back_buf,
    ret_buf,
    w_sem,
    send_sem,
    recv_sem,
    send2_sem,
    recv2_sem,
):
    inner_size, outer_size = sizes
    peers = inner_size * outer_size
    rows, width = hidden_hbm.shape
    chunks, _, count, _ = out_buf.shape
    size = rows // chunks
    head = width // HEADS
    channels = final_hbm.shape[0]
    tiles = width // LANES
    inner = lax.axis_index("inner")
    outer = lax.axis_index("outer")
    me = inner * outer_size + outer

    far = outer_size // 2 if outer_size % 2 == 0 else 0

    def outer_of(j):
        span = outer_size - far
        side = outer // span
        crossing = (1 - side) * far + lax.rem(outer + j, span)
        same = side * span + lax.rem(outer + j - far, span)
        return jnp.where(j < far, crossing, same)

    def fetch(source, target, index, lo, hi):
        return pltpu.make_async_copy(
            source.at[:, lo:hi], target.at[:, lo:hi], w_sem.at[index]
        )

    loads = [
        fetch(time_hbm, time_w, 0, 0, 2 * width),
        fetch(sqkv_hbm, sqkv_w, 1, width, 2 * width),
        fetch(sqkv_hbm, sqkv_w, 2, 2 * width, 3 * width),
        fetch(sqkv_hbm, sqkv_w, 3, 0, width),
        fetch(time_hbm, time_w, 4, 2 * width, 6 * width),
        fetch(sout_hbm, sout_w, 5, 0, width),
        fetch(tqkv_hbm, tqkv_w, 6, 0, 3 * width),
        fetch(tout_hbm, tout_w, 7, 0, width),
    ]
    rest = [
        pltpu.make_async_copy(now_hbm, now_ref, w_sem.at[9]),
        pltpu.make_async_copy(next_hbm, next_ref, w_sem.at[10]),
        pltpu.make_async_copy(final_hbm, final_ref, w_sem.at[11]),
        pltpu.make_async_copy(tag_hbm, tag_ref, w_sem.at[12]),
        pltpu.make_async_copy(level_hbm, level_ref, w_sem.at[13]),
    ]
    hidden_load = pltpu.make_async_copy(hidden_hbm, hidden_ref, w_sem.at[8])
    step_load = pltpu.make_async_copy(step_hbm, step_ref, w_sem.at[14])
    step_load.start()
    loads[0].start()
    hidden_load.start()
    for load in loads[1:6]:
        load.start()

    barrier = pltpu.get_barrier_semaphore()

    @pl.loop(1, peers)
    def _(k):
        peer = lax.rem(me + k, peers)
        pl.semaphore_signal(
            barrier,
            inc=1,
            device_id=(peer // outer_size, lax.rem(peer, outer_size)),
            device_id_type=MESH,
        )

    feature = lax.broadcasted_iota(jnp.int32, (width, LANES), 0)
    column = lax.broadcasted_iota(jnp.int32, (width, LANES), 1) * head
    group_ref[...] = jnp.where(
        (feature >= column) & (feature < column + head), 1.0, 0.0
    ).astype(bf16)
    feature = lax.broadcasted_iota(jnp.int32, (LANES, width), 1)
    column = lax.broadcasted_iota(jnp.int32, (LANES, width), 0) * head
    spread = jnp.where((feature >= column) & (feature < column + head), 1.0, 0.0).astype(bf16)
    spread_ref[0:LANES, :] = spread
    spread_ref[LANES:, :] = spread

    step_load.wait()
    time_value = jnp.full((8, LANES), step_ref[0].astype(f32)) / STEPS
    lane = lax.broadcasted_iota(jnp.int32, (8, LANES), 1).astype(f32)
    angles = 1000.0 * time_value * jnp.exp(-math.log(10000.0) * lane / LANES)
    embedded = jnp.concatenate([jnp.cos(angles), jnp.sin(angles)], 1)
    activated = (embedded / (1.0 + jnp.exp(-embedded))).astype(bf16)
    loads[0].wait()
    table[:, 0 : 2 * width] = dot(activated, time_w[:, 0 : 2 * width])

    def entry(index):
        return table[0:1, index * width : (index + 1) * width]

    hidden_load.wait()
    hidden = hidden_ref[...].astype(f32)
    normed = (layer_norm(hidden) * (1.0 + entry(1)) + entry(0)).astype(bf16)

    def head_norm(values, factor):
        total = dot((values * values).astype(bf16), group_ref[...])
        inverse = lax.rsqrt(total / head + norm_eps) * factor
        high, low = split_pair(inverse)
        return (values * dot(jnp.concatenate([high, low], 1), spread_ref[...])).astype(bf16)

    lane_id = lax.broadcasted_iota(jnp.int32, (1, WINDOW), 1)

    def own_lanes(index, tile):
        inside = (lane_id >= index * head - tile * LANES) & (
            lane_id < (index + 1) * head - tile * LANES
        )
        return jnp.where(inside, 1.0, 0.0).astype(bf16)

    def window_of(index):
        tile = min(index * head // LANES, (width - WINDOW) // LANES)
        return tile, slice(tile * LANES, tile * LANES + WINDOW)

    def attend_spatial(queries):
        tops, bottoms = [None] * tiles, [None] * tiles
        for first in range(0, HEADS, GROUP):
            group = range(first, first + GROUP)
            scores = []
            for index in group:
                tile, window = window_of(index)
                own = own_lanes(index, tile)
                scores.append(dot_t(queries[:, window] * own, k_ref[:, window]))
            weights = [jnp.exp(score).astype(bf16) for score in scores]
            for index, weight in zip(group, weights):
                tile, window = window_of(index)
                own = own_lanes(index, tile)
                mixed = dot(weight, v_ref[:, window] * own + (1.0 - own))
                for side in range(WINDOW // LANES):
                    begin = index * head - (tile + side) * LANES
                    if begin >= LANES or begin + head <= 0:
                        continue
                    top = mixed[:, side * LANES : (side + 1) * LANES]
                    bottom = mixed[:, (1 - side) * LANES : (2 - side) * LANES]
                    here = tile + side
                    if tops[here] is None:
                        tops[here], bottoms[here] = top, bottom
                    else:
                        short = lane_id[:, :LANES] >= begin
                        tops[here] = jnp.where(short, top, tops[here])
                        bottoms[here] = jnp.where(short, bottom, bottoms[here])
        return jnp.concatenate(
            [(top / bottom).astype(bf16) for top, bottom in zip(tops, bottoms)], 1
        )

    def attend_temporal(queries, keys, values):
        tops, bottoms = [None] * tiles, [None] * tiles

        def add(parts, here, part):
            parts[here] = part if parts[here] is None else parts[here] + part

        for index in range(0, HEADS, 2):
            tile, window = window_of(index)
            pair = [own_lanes(index, tile), own_lanes(index + 1, tile)]
            key = keys[:, window]
            score = dot_t(queries[:, window], jnp.concatenate([key * own for own in pair], 0))
            weight = jnp.exp(score).astype(bf16) * mask_ref[...]
            value = values[:, window]
            top = dot(weight, jnp.concatenate([value * own for own in pair], 0))
            ones = [jnp.broadcast_to(own, (size, WINDOW)) for own in pair]
            bottom = dot(weight, jnp.concatenate(ones, 0))
            for side in range(WINDOW // LANES):
                lanes = slice(side * LANES, (side + 1) * LANES)
                add(tops, tile + side, top[:, lanes])
                add(bottoms, tile + side, bottom[:, lanes])
        return jnp.concatenate(
            [(top / bottom).astype(bf16) for top, bottom in zip(tops, bottoms)], 1
        )

    loads[1].wait()
    k_ref[...] = head_norm(dot(normed, sqkv_w[:, width : 2 * width]), 1.0)
    loads[2].wait()
    v_ref[...] = dot(normed, sqkv_w[:, 2 * width : 3 * width]).astype(bf16)
    loads[3].wait()
    loads[6].start()
    loads[7].start()
    for load in rest:
        load.start()
    loads[4].wait()
    table[:, 2 * width :] = dot(activated, time_w[:, 2 * width :])
    loads[5].wait()

    def forward(chunk, inner_id, outer_id):
        return pltpu.make_async_remote_copy(
            src_ref=out_buf.at[chunk, inner_id * outer_size + outer_id],
            dst_ref=in_buf.at[chunk, me],
            send_sem=send_sem.at[chunk],
            recv_sem=recv_sem.at[chunk],
            device_id=(inner_id, outer_id),
            device_id_type=MESH,
        )

    def backward(chunk, inner_id, outer_id):
        return pltpu.make_async_remote_copy(
            src_ref=back_buf.at[chunk, inner_id * outer_size + outer_id],
            dst_ref=ret_buf.at[chunk, me],
            send_sem=send2_sem.at[chunk],
            recv_sem=recv2_sem.at[chunk],
            device_id=(inner_id, outer_id),
            device_id_type=MESH,
        )

    def everyone(chunk, source, target, sends, receives):
        return pltpu.make_async_remote_copy(
            src_ref=source.at[chunk, pl.ds(0, peers - 1)],
            dst_ref=target.at[chunk, pl.ds(0, peers - 1)],
            send_sem=sends.at[chunk],
            recv_sem=receives.at[chunk],
            device_id=(inner, outer),
            device_id_type=MESH,
        )

    own_turn = far * inner_size

    def exchange(copy, chunk):
        def send(k):
            to_inner = lax.rem(inner + lax.rem(k, inner_size), inner_size)
            copy(chunk, to_inner, outer_of(k // inner_size)).start()

        @pl.loop(0, own_turn)
        def _(k):
            send(k)

        @pl.loop(own_turn + 1, peers)
        def _(k):
            send(k)

    for chunk in range(chunks):
        lo = chunk * size
        queries = head_norm(dot(normed[lo : lo + size], sqkv_w[:, 0:width]), head**-0.5)
        attended = attend_spatial(queries)
        projected = dot(attended, sout_w[...])
        after = hidden_ref[lo : lo + size, :].astype(f32) + entry(2) * projected
        out_buf[chunk] = after.reshape(peers, count, width).astype(bf16)
        if chunk == 0:
            pl.semaphore_wait(barrier, peers - 1)
        exchange(forward, chunk)
        in_buf[chunk, me] = out_buf[chunk, me]

    place = lax.rem(lax.broadcasted_iota(jnp.int32, (size, 2 * size), 0), count)
    other = lax.rem(lax.broadcasted_iota(jnp.int32, (size, 2 * size), 1), count)
    mask_ref[...] = jnp.where(place == other, 1.0, 0.0).astype(bf16)
    slot = lax.rem(lax.broadcasted_iota(jnp.int32, (size, LANES), 0), count)
    own_slot = slot == lax.broadcasted_iota(jnp.int32, (size, LANES), 1) // channels
    loads[6].wait()
    loads[7].wait()
    for load in rest:
        load.wait()
    repeated = jnp.concatenate([final_ref[...]] * (LANES // channels), 0)

    for chunk in range(chunks):
        everyone(chunk, out_buf, in_buf, send_sem, recv_sem).wait_recv()
        after = in_buf[chunk].astype(f32).reshape(size, width)
        normed = (layer_norm(after) * (1.0 + entry(4)) + entry(3)).astype(bf16)
        queries = head_norm(dot(normed, tqkv_w[:, 0:width]), head**-0.5)
        keys = head_norm(dot(normed, tqkv_w[:, width : 2 * width]), 1.0)
        values = dot(normed, tqkv_w[:, 2 * width :]).astype(bf16)
        attended = attend_temporal(queries, keys, values)
        term = dot(attended, tout_w[...]).astype(bf16).astype(f32)
        after = in_buf[chunk].astype(f32).reshape(size, width)
        final_normed = layer_norm(after + entry(5) * term).astype(bf16)
        mixed = jnp.where(own_slot, dot_t(final_normed, repeated), 0.0)
        packed = jnp.sum(mixed.reshape(peers, count, LANES), 1)
        back_buf[chunk] = packed.reshape(peers, 1, LANES)
        exchange(backward, chunk)
        ret_buf[chunk, me] = back_buf[chunk, me]

    level = jnp.float32(0.0)
    for version in range(level_ref.shape[0]):
        level = level + jnp.where(tag_ref[0] == version, level_ref[version], 0.0)
    time_row = jnp.full((1, rows), step_ref[0].astype(f32)) / STEPS
    noise_scale = level * jnp.sqrt(time_row / (1.0 - time_row))
    factor = noise_scale * noise_scale / (2.0 * time_row)
    deviation = noise_scale * math.sqrt(1.0 / STEPS)
    lane = lax.broadcasted_iota(jnp.int32, (channels, LANES), 1)
    pick = lax.rem(lane, channels) == lax.broadcasted_iota(jnp.int32, (channels, LANES), 0)
    pick = jnp.where(pick, 1.0, 0.0).astype(bf16)
    for chunk in range(chunks):
        everyone(chunk, out_buf, in_buf, send_sem, recv_sem).wait_send()

    velocity = []
    for chunk in range(chunks):
        everyone(chunk, back_buf, ret_buf, send2_sem, recv2_sem).wait_recv()
        packed = jnp.broadcast_to(ret_buf[chunk], (peers, count, LANES)).reshape(size, LANES)
        packed = jnp.where(own_slot, packed, 0.0)
        high = packed.astype(bf16)
        residue = packed - high.astype(f32)
        middle = residue.astype(bf16)
        low = (residue - middle.astype(f32)).astype(bf16)
        velocity.append(dot_t(pick, high) + dot_t(pick, middle) + dot_t(pick, low))
    velocity = jnp.concatenate(velocity, 1)
    now = now_ref[0]
    drift = velocity + factor * (now + (1.0 - time_row) * velocity)
    next_mean = now - drift / STEPS
    mean_ref[0] = next_mean
    standard = (next_ref[0] - next_mean) / deviation
    logp_ref[...] = (
        -0.5 * jnp.mean(standard * standard, 0, keepdims=True)
        - jnp.log(deviation)
        - 0.5 * math.log(2.0 * math.pi)
    )
    for chunk in range(chunks):
        everyone(chunk, back_buf, ret_buf, send2_sem, recv2_sem).wait_send()


def shards(sizes, hidden, now, following, step, tags, levels, time_w, sqkv, sout, tqkv, tout, final):
    peers = sizes[0] * sizes[1]
    rows, width = hidden.shape
    count = rows // peers
    chunks = 2 if count % 2 == 0 else 1
    size = rows // chunks
    vmem = pl.BlockSpec(memory_space=pltpu.VMEM)
    hbm = pl.BlockSpec(memory_space=pl.ANY)
    exchange = pltpu.VMEM((chunks, peers, count // chunks, width), bf16)
    returned = pltpu.VMEM((chunks, peers, 1, LANES), f32)
    sems = pltpu.SemaphoreType.DMA((chunks,))
    return pl.pallas_call(
        functools.partial(kernel, sizes),
        out_shape=(pltpu.VMEM((1, rows), f32), pltpu.VMEM(now.shape, f32)),
        in_specs=[hbm] * 12,
        out_specs=(vmem, vmem),
        scratch_shapes=[
            pltpu.SMEM(step.shape, step.dtype),
            pltpu.SMEM(tags.shape, tags.dtype),
            pltpu.SMEM(levels.shape, levels.dtype),
            pltpu.VMEM(hidden.shape, bf16),
            pltpu.VMEM(now.shape, f32),
            pltpu.VMEM(following.shape, f32),
            pltpu.VMEM(final.shape, bf16),
            pltpu.VMEM(time_w.shape, bf16),
            pltpu.VMEM(sqkv.shape, bf16),
            pltpu.VMEM(sout.shape, bf16),
            pltpu.VMEM(tqkv.shape, bf16),
            pltpu.VMEM(tout.shape, bf16),
            pltpu.VMEM((8, 6 * width), f32),
            pltpu.VMEM((width, LANES), bf16),
            pltpu.VMEM((2 * LANES, width), bf16),
            pltpu.VMEM((size, 2 * size), bf16),
            pltpu.VMEM((rows, width), bf16),
            pltpu.VMEM((rows, width), bf16),
            exchange,
            exchange,
            returned,
            returned,
            pltpu.SemaphoreType.DMA((15,)),
            sems,
            sems,
            sems,
            sems,
        ],
        compiler_params=pltpu.CompilerParams(
            collective_id=0, has_side_effects=True, vmem_limit_bytes=60 * 1024 * 1024
        ),
    )(hidden, now, following, step, tags, levels, final, time_w, sqkv, sout, tqkv, tout)


def solution(mesh):
    split = P(("inner", "outer"), None)
    split3 = P(("inner", "outer"), None, None)
    sizes = (mesh.shape["inner"], mesh.shape["outer"])
    return jax.shard_map(
        functools.partial(shards, sizes),
        mesh=mesh,
        in_specs=(split, split3, split3, P(), P(("inner", "outer")))
        + (P(),) * 7,
        out_specs=(split, split3),
        check_vma=False,
    )
```

time: 48.9 us -> 39.9 us (0.82)
  Pallas kernels: 45.6 us -> 36.7 us
    pallas_call x1, Pallas kernels: 45.6 us -> 36.7 us  [shards(): pl.pallas_call(functools.partial(kernel, sizes), out_shape=(pltpu.VMEM((1...]
where the time goes in v2:
time: 39.9 us; the launch traced here: 39.8 us
  Pallas kernels  36.7 us (92%)
  between operations  1.93 us (5%)
  local copies, waits for them, and re-layouts  1.17 us (3%)
    pallas_call x1, Pallas kernels, shards(): pl.pallas_call(functools.partial(kernel, sizes), out_shape=(pltpu.VMEM((1...  36.7 us
    unnamed x2, local copies, waits for them, and re-layouts  1.17 us

profile of v2, /device:TPU:0, one launch (start us, length us, event | category | flops | bytes accessed | tf_op | source)
XLA Modules:
  0.0 39.8 jit_solution(6154461091457756893)
XLA Ops:
  1.9 36.7 %shard_map.131 = (f32[1,256]{1,0:T(1,128)S(1)}, f32[1,16,256]{2,1,0:T(8,128)S(1)}) custom-call(bf16[256,1152]{1,0:T(8,128)(2,1)} %hidden_hbm.1, f32[1,16,256]{2,1,0:T(8,128)} %now_hbm.1, f32[1,16,256]{2,1,0:T(8,128)} %next_hbm.1, s32[1]{0:T(128)S(6)} %copy.18.step_hbm, s32[1]{0:T(128)S(6)} %copy.19.tag_hbm, f32[8]{0:T(128)} %level_hbm.1, ...), custom_call_target="tpu_custom_call" | custom-call | tf_op jit(solution)/shard_map/pallas_call | solution.py:396
  38.6 0.6 %copy.16 = f32[1,256]{1,0:T(1,128)} copy(f32[1,256]{1,0:T(1,128)S(1)} %get-tuple-element.2) | data formatting | bytes 2048
  39.2 0.6 %copy.17 = f32[1,16,256]{2,1,0:T(8,128)} copy(f32[1,16,256]{2,1,0:T(8,128)S(1)} %get-tuple-element.3) | data formatting | bytes 32768

commit v3 on v2

v3 whole, which is shorter than its diff:
```python
import functools
import math

import jax
import jax.numpy as jnp
from jax import lax
from jax.experimental import pallas as pl
from jax.experimental.pallas import tpu as pltpu
from jax.sharding import PartitionSpec as P

HEADS = 16
STEPS = 10
LANES = 128
WINDOW = 256
GROUP = 8
norm_eps = 1e-06
f32 = jnp.float32
bf16 = jnp.bfloat16
MESH = pl.DeviceIdType.MESH


def layer_norm(values):
    average = jnp.mean(values, -1, keepdims=True)
    centred = values - average
    variance = jnp.mean(centred * centred, -1, keepdims=True)
    return centred * lax.rsqrt(variance + norm_eps)


def split_pair(values):
    high = values.astype(bf16)
    return high, (values - high.astype(f32)).astype(bf16)


def dot(a, b):
    return jnp.dot(a, b, preferred_element_type=f32)


def dot_t(a, b):
    return lax.dot_general(a, b, (((1,), (1,)), ((), ())), preferred_element_type=f32)


def kernel(
    sizes,
    hidden_hbm,
    now_hbm,
    next_hbm,
    step_hbm,
    tag_hbm,
    level_hbm,
    final_hbm,
    time_hbm,
    sqkv_hbm,
    sout_hbm,
    tqkv_hbm,
    tout_hbm,
    logp_ref,
    mean_ref,
    step_ref,
    tag_ref,
    level_ref,
    hidden_ref,
    now_ref,
    next_ref,
    final_ref,
    time_w,
    sqkv_w,
    sout_w,
    tqkv_w,
    tout_w,
    table,
    group_ref,
    spread_ref,
    mask_ref,
    after_ref,
    q_ref,
    k_ref,
    v_ref,
    out_buf,
    in_buf,
    back_buf,
    ret_buf,
    w_sem,
    send_sem,
    recv_sem,
    send2_sem,
    recv2_sem,
):
    inner_size, outer_size = sizes
    peers = inner_size * outer_size
    rows, width = hidden_hbm.shape
    count = rows // peers
    chunks = 2 if inner_size % 2 == 0 else 1
    halves = 2 if outer_size % 2 == 0 else 1
    span = outer_size // halves
    block_peers = peers // halves
    size = rows // chunks
    part = rows // halves
    each = inner_size // chunks
    head = width // HEADS
    channels = final_hbm.shape[0]
    tiles = width // LANES
    inner = lax.axis_index("inner")
    outer = lax.axis_index("outer")
    me = inner * outer_size + outer
    core = lax.rem(inner, chunks)

    side = outer // span

    def slot_of(inner_id, outer_id):
        return outer_id * inner_size + inner_id

    def block_of(inner_id, outer_id):
        return (lax.rem(inner_id, chunks) * outer_size + outer_id) * each + inner_id // chunks

    my_slot = slot_of(inner, outer)
    my_block = block_of(inner, outer)

    early = -(-tiles // 2) * LANES

    def fetch(source, target, index, lo, hi):
        return pltpu.make_async_copy(
            source.at[:, lo:hi], target.at[:, lo:hi], w_sem.at[index]
        )

    loads = [
        fetch(time_hbm, time_w, 0, 0, 2 * width),
        fetch(sqkv_hbm, sqkv_w, 1, width, width + early),
        fetch(sqkv_hbm, sqkv_w, 2, 2 * width, 3 * width),
        fetch(sqkv_hbm, sqkv_w, 3, 0, width),
        fetch(time_hbm, time_w, 4, 2 * width, 3 * width),
        fetch(sout_hbm, sout_w, 5, 0, width),
        fetch(tqkv_hbm, tqkv_w, 6, 0, 3 * width),
        fetch(tout_hbm, tout_w, 7, 0, width),
        fetch(sqkv_hbm, sqkv_w, 15, width + early, 2 * width),
        fetch(time_hbm, time_w, 16, 3 * width, 6 * width),
    ]
    rest = [
        pltpu.make_async_copy(now_hbm, now_ref, w_sem.at[9]),
        pltpu.make_async_copy(next_hbm, next_ref, w_sem.at[10]),
        pltpu.make_async_copy(final_hbm, final_ref, w_sem.at[11]),
        pltpu.make_async_copy(tag_hbm, tag_ref, w_sem.at[12]),
        pltpu.make_async_copy(level_hbm, level_ref, w_sem.at[13]),
    ]
    hidden_load = pltpu.make_async_copy(hidden_hbm, hidden_ref, w_sem.at[8])
    step_load = pltpu.make_async_copy(step_hbm, step_ref, w_sem.at[14])
    step_load.start()
    hidden_load.start()
    loads[0].start()
    for index in (1, 8, 2, 3, 5, 4, 6, 7, 9):
        loads[index].start()
    for load in rest:
        load.start()

    barrier = pltpu.get_barrier_semaphore()

    def wrap(value, bound):
        return jnp.where(value >= bound, value - bound, value)

    for turn in range(outer_size):
        to_outer = wrap(outer + turn, outer_size)

        @pl.loop(1 if turn == 0 else 0, inner_size)
        def _(k):
            pl.semaphore_signal(
                barrier,
                inc=1,
                device_id=(wrap(inner + k, inner_size), to_outer),
                device_id_type=MESH,
            )

    feature = lax.broadcasted_iota(jnp.int32, (width, LANES), 0)
    column = lax.broadcasted_iota(jnp.int32, (width, LANES), 1) * head
    group_ref[...] = jnp.where(
        (feature >= column) & (feature < column + head), 1.0, 0.0
    ).astype(bf16)
    feature = lax.broadcasted_iota(jnp.int32, (LANES, width), 1)
    column = lax.broadcasted_iota(jnp.int32, (LANES, width), 0) * head
    spread = jnp.where((feature >= column) & (feature < column + head), 1.0, 0.0).astype(bf16)
    spread_ref[0:LANES, :] = spread
    spread_ref[LANES:, :] = spread

    step_load.wait()
    time_value = jnp.full((8, LANES), step_ref[0].astype(f32)) / STEPS
    lane = lax.broadcasted_iota(jnp.int32, (8, LANES), 1).astype(f32)
    angles = 1000.0 * time_value * jnp.exp(-math.log(10000.0) * lane / LANES)
    embedded = jnp.concatenate([jnp.cos(angles), jnp.sin(angles)], 1)
    activated = (embedded / (1.0 + jnp.exp(-embedded))).astype(bf16)
    hidden_load.wait()
    standard = layer_norm(hidden_ref[...].astype(f32))
    loads[0].wait()
    table[:, 0 : 2 * width] = dot(activated, time_w[:, 0 : 2 * width])

    def entry(index):
        return table[0:1, index * width : (index + 1) * width]

    normed = (standard * (1.0 + entry(1)) + entry(0)).astype(bf16)

    def head_norm(values, factor):
        total = dot((values * values).astype(bf16), group_ref[...])
        inverse = lax.rsqrt(total / head + norm_eps) * factor
        high, low = split_pair(inverse)
        return (values * dot(jnp.concatenate([high, low], 1), spread_ref[...])).astype(bf16)

    lane_id = lax.broadcasted_iota(jnp.int32, (1, WINDOW), 1)

    def own_lanes(index, tile):
        inside = (lane_id >= index * head - tile * LANES) & (
            lane_id < (index + 1) * head - tile * LANES
        )
        return jnp.where(inside, 1.0, 0.0).astype(bf16)

    def window_of(index):
        tile = min(index * head // LANES, (width - WINDOW) // LANES)
        return tile, slice(tile * LANES, tile * LANES + WINDOW)

    def attend(queries, masked):
        tops, bottoms = [None] * tiles, [None] * tiles
        for first in range(0, HEADS, GROUP):
            group = range(first, first + GROUP)
            scores = []
            for index in group:
                tile, window = window_of(index)
                own = own_lanes(index, tile)
                scores.append(dot_t(queries[:, window] * own, k_ref[:, window]))
            weights = [jnp.exp(score).astype(bf16) for score in scores]
            if masked:
                weights = [weight * mask_ref[...] for weight in weights]
            for index, weight in zip(group, weights):
                tile, window = window_of(index)
                own = own_lanes(index, tile)
                mixed = dot(weight, v_ref[:, window] * own + (1.0 - own))
                for side in range(WINDOW // LANES):
                    begin = index * head - (tile + side) * LANES
                    if begin >= LANES or begin + head <= 0:
                        continue
                    top = mixed[:, side * LANES : (side + 1) * LANES]
                    bottom = mixed[:, (1 - side) * LANES : (2 - side) * LANES]
                    here = tile + side
                    if tops[here] is None:
                        tops[here], bottoms[here] = top, bottom
                    else:
                        short = lane_id[:, :LANES] >= begin
                        tops[here] = jnp.where(short, top, tops[here])
                        bottoms[here] = jnp.where(short, bottom, bottoms[here])
        return jnp.concatenate(
            [(top / bottom).astype(bf16) for top, bottom in zip(tops, bottoms)], 1
        )

    loads[1].wait()
    first = dot(normed, sqkv_w[:, width : width + early])
    loads[8].wait()
    second = dot(normed, sqkv_w[:, width + early : 2 * width])
    k_ref[...] = head_norm(jnp.concatenate([first, second], 1), 1.0)
    loads[2].wait()
    v_ref[...] = dot(normed, sqkv_w[:, 2 * width : 3 * width]).astype(bf16)
    loads[3].wait()

    def forward(inner_id, outer_id, chunk, turn):
        return pltpu.make_async_remote_copy(
            src_ref=out_buf.at[block_of(inner_id, outer_id)],
            dst_ref=in_buf.at[my_slot],
            send_sem=send_sem.at[chunk, turn],
            recv_sem=recv_sem.at[turn],
            device_id=(inner_id, outer_id),
            device_id_type=MESH,
        )

    def backward(inner_id, outer_id, turn):
        return pltpu.make_async_remote_copy(
            src_ref=back_buf.at[slot_of(inner_id, outer_id)],
            dst_ref=ret_buf.at[my_block],
            send_sem=send2_sem.at[turn],
            recv_sem=recv2_sem.at[turn],
            device_id=(inner_id, outer_id),
            device_id_type=MESH,
        )

    def partners(turn):
        return block_peers - (1 if turn == halves - 1 else 0)

    def several(source, target, sends, receives, blocks):
        return pltpu.make_async_remote_copy(
            src_ref=source.at[pl.ds(0, blocks)],
            dst_ref=target.at[pl.ds(0, blocks)],
            send_sem=sends,
            recv_sem=receives,
            device_id=(inner, outer),
            device_id_type=MESH,
        )

    def half_of(turn):
        return lax.rem(side + 1 + turn, halves)

    place = outer - side * span

    def send(chunk, turn):
        for step in range(span):
            to_outer = half_of(turn) * span + wrap(place + step, span)

            def start(k):
                to_inner = wrap(inner // chunks + k, each) * chunks + chunk
                forward(to_inner, to_outer, chunk, turn).start()

            if turn == halves - 1 and step == 0:

                @pl.when(core != chunk)
                def _():
                    start(0)

                pl.loop(1, each)(start)
            else:
                pl.loop(0, each)(start)

    for chunk in range(chunks):
        lo = chunk * size
        queries = head_norm(dot(normed[lo : lo + size], sqkv_w[:, 0:width]), head**-0.5)
        attended = attend(queries, False)
        if chunk == 0:
            loads[5].wait()
            loads[4].wait()
            table[:, 2 * width : 3 * width] = dot(activated, time_w[:, 2 * width : 3 * width])
        projected = dot(attended, sout_w[...])
        after = hidden_ref[lo : lo + size, :].astype(f32) + entry(2) * projected
        out_buf[chunk * outer_size * each : (chunk + 1) * outer_size * each] = after.reshape(
            outer_size * each, count, width
        ).astype(bf16)
        if chunk == 0:
            pl.semaphore_wait(barrier, peers - 1)
        for turn in range(halves) if chunk == 0 else reversed(range(halves)):
            send(chunk, turn)
    in_buf[my_slot] = out_buf[my_block]

    loads[9].wait()
    table[:, 3 * width :] = dot(activated, time_w[:, 3 * width :])
    row = lax.rem(lax.broadcasted_iota(jnp.int32, (rows, rows), 0), count)
    other = lax.rem(lax.broadcasted_iota(jnp.int32, (rows, rows), 1), count)
    mask_ref[...] = jnp.where(row == other, 1.0, 0.0).astype(bf16)
    slot = lax.rem(lax.broadcasted_iota(jnp.int32, (rows, LANES), 0), count)
    own_slot = slot == lax.broadcasted_iota(jnp.int32, (rows, LANES), 1) // channels
    loads[6].wait()
    loads[7].wait()
    for load in rest:
        load.wait()
    repeated = jnp.concatenate([final_ref[...]] * (LANES // channels), 0)

    for turn in reversed(range(halves)):
        lo = (halves - 1 - turn) * part
        several(out_buf, in_buf, send_sem.at[0, turn], recv_sem.at[turn], partners(turn)).wait_recv()
        after = in_buf[pl.ds(half_of(turn) * block_peers, block_peers)]
        after = after.astype(f32).reshape(part, width)
        normed = (layer_norm(after) * (1.0 + entry(4)) + entry(3)).astype(bf16)
        after_ref[lo : lo + part, :] = after.astype(bf16)
        q_ref[lo : lo + part, :] = head_norm(dot(normed, tqkv_w[:, 0:width]), head**-0.5)
        k_ref[lo : lo + part, :] = head_norm(dot(normed, tqkv_w[:, width : 2 * width]), 1.0)
        v_ref[lo : lo + part, :] = dot(normed, tqkv_w[:, 2 * width :]).astype(bf16)
    attended = attend(q_ref, True)
    term = dot(attended, tout_w[...]).astype(bf16).astype(f32)
    final_normed = layer_norm(after_ref[...].astype(f32) + entry(5) * term).astype(bf16)
    mixed = jnp.where(own_slot, dot_t(final_normed, repeated), 0.0)
    packed = jnp.sum(mixed.reshape(peers, count, LANES), 1)
    packed = packed.reshape(peers, 1, LANES)
    for turn in range(halves):
        order = halves - 1 - turn
        back_buf[pl.ds(half_of(turn) * block_peers, block_peers)] = packed[
            order * block_peers : (order + 1) * block_peers
        ]
    for turn in range(halves):

        for step in range(span):
            to_outer = half_of(turn) * span + wrap(place + step, span)

            @pl.loop(1 if turn == halves - 1 and step == 0 else 0, inner_size)
            def _(k):
                backward(wrap(inner + k, inner_size), to_outer, turn).start()

    ret_buf[my_block] = back_buf[my_slot]

    level = jnp.float32(0.0)
    for version in range(level_ref.shape[0]):
        level = level + jnp.where(tag_ref[0] == version, level_ref[version], 0.0)
    time_row = jnp.full((1, rows), step_ref[0].astype(f32)) / STEPS
    noise_scale = level * jnp.sqrt(time_row / (1.0 - time_row))
    factor = noise_scale * noise_scale / (2.0 * time_row)
    deviation = noise_scale * math.sqrt(1.0 / STEPS)
    lane = lax.broadcasted_iota(jnp.int32, (channels, LANES), 1)
    pick = lax.rem(lane, channels) == lax.broadcasted_iota(jnp.int32, (channels, LANES), 0)
    pick = jnp.where(pick, 1.0, 0.0).astype(bf16)
    for chunk in range(chunks):
        for turn in range(halves - 1):
            several(out_buf, in_buf, send_sem.at[chunk, turn], recv_sem.at[0], span * each).wait_send()
        last = halves - 1

        @pl.when(core != chunk)
        def _():
            several(out_buf, in_buf, send_sem.at[chunk, last], recv_sem.at[0], span * each).wait_send()

        @pl.when(core == chunk)
        def _():
            several(out_buf, in_buf, send_sem.at[chunk, last], recv_sem.at[0], span * each - 1).wait_send()

    for turn in range(halves):
        several(
            back_buf, ret_buf, send2_sem.at[turn], recv2_sem.at[turn], partners(turn)
        ).wait_recv()
    packed = jnp.broadcast_to(ret_buf[...], (peers, count, LANES)).reshape(rows, LANES)
    packed = jnp.where(own_slot, packed, 0.0)
    high = packed.astype(bf16)
    residue = packed - high.astype(f32)
    middle = residue.astype(bf16)
    low = (residue - middle.astype(f32)).astype(bf16)
    velocity = dot_t(pick, high) + dot_t(pick, middle) + dot_t(pick, low)
    now = now_ref[0]
    drift = velocity + factor * (now + (1.0 - time_row) * velocity)
    next_mean = now - drift / STEPS
    mean_ref[0] = next_mean
    standard = (next_ref[0] - next_mean) / deviation
    logp_ref[...] = (
        -0.5 * jnp.mean(standard * standard, 0, keepdims=True)
        - jnp.log(deviation)
        - 0.5 * math.log(2.0 * math.pi)
    )
    for turn in range(halves):
        several(
            back_buf, ret_buf, send2_sem.at[turn], recv2_sem.at[turn], partners(turn)
        ).wait_send()


def shards(sizes, hidden, now, following, step, tags, levels, time_w, sqkv, sout, tqkv, tout, final):
    peers = sizes[0] * sizes[1]
    rows, width = hidden.shape
    count = rows // peers
    vmem = pl.BlockSpec(memory_space=pltpu.VMEM)
    hbm = pl.BlockSpec(memory_space=pl.ANY)
    exchange = pltpu.VMEM((peers, count, width), bf16)
    returned = pltpu.VMEM((peers, 1, LANES), f32)
    sems = pltpu.SemaphoreType.DMA((2,))
    return pl.pallas_call(
        functools.partial(kernel, sizes),
        out_shape=(pltpu.VMEM((1, rows), f32), pltpu.VMEM(now.shape, f32)),
        in_specs=[hbm] * 12,
        out_specs=(vmem, vmem),
        scratch_shapes=[
            pltpu.SMEM(step.shape, step.dtype),
            pltpu.SMEM(tags.shape, tags.dtype),
            pltpu.SMEM(levels.shape, levels.dtype),
            pltpu.VMEM(hidden.shape, bf16),
            pltpu.VMEM(now.shape, f32),
            pltpu.VMEM(following.shape, f32),
            pltpu.VMEM(final.shape, bf16),
            pltpu.VMEM(time_w.shape, bf16),
            pltpu.VMEM(sqkv.shape, bf16),
            pltpu.VMEM(sout.shape, bf16),
            pltpu.VMEM(tqkv.shape, bf16),
            pltpu.VMEM(tout.shape, bf16),
            pltpu.VMEM((8, 6 * width), f32),
            pltpu.VMEM((width, LANES), bf16),
            pltpu.VMEM((2 * LANES, width), bf16),
            pltpu.VMEM((rows, rows), bf16),
            pltpu.VMEM((rows, width), bf16),
            pltpu.VMEM((rows, width), bf16),
            pltpu.VMEM((rows, width), bf16),
            pltpu.VMEM((rows, width), bf16),
            exchange,
            exchange,
            returned,
            returned,
            pltpu.SemaphoreType.DMA((17,)),
            pltpu.SemaphoreType.DMA((2, 2)),
            sems,
            sems,
            sems,
        ],
        compiler_params=pltpu.CompilerParams(
            collective_id=0, has_side_effects=True, vmem_limit_bytes=60 * 1024 * 1024
        ),
    )(hidden, now, following, step, tags, levels, final, time_w, sqkv, sout, tqkv, tout)


def solution(mesh):
    split = P(("inner", "outer"), None)
    split3 = P(("inner", "outer"), None, None)
    sizes = (mesh.shape["inner"], mesh.shape["outer"])
    return jax.shard_map(
        functools.partial(shards, sizes),
        mesh=mesh,
        in_specs=(split, split3, split3, P(), P(("inner", "outer")))
        + (P(),) * 7,
        out_specs=(split, split3),
        check_vma=False,
    )
```

time: 39.9 us -> 37.1 us (0.930)
  Pallas kernels: 36.7 us -> 33.8 us
    pallas_call x1, Pallas kernels: 36.7 us -> 33.8 us  [shards(): pl.pallas_call(functools.partial(kernel, sizes), out_shape=(pltpu.VMEM((1...]
where the time goes in v3:
time: 37.1 us; the launch traced here: 36.9 us
  Pallas kernels  33.8 us (91%)
  between operations  1.93 us (5%)
  local copies, waits for them, and re-layouts  1.17 us (3%)
    pallas_call x1, Pallas kernels, shards(): pl.pallas_call(functools.partial(kernel, sizes), out_shape=(pltpu.VMEM((1...  33.8 us
    unnamed x2, local copies, waits for them, and re-layouts  1.17 us

profile of v3, /device:TPU:0, one launch (start us, length us, event | category | flops | bytes accessed | tf_op | source)
XLA Modules:
  0.0 36.9 jit_solution(6800480489249206766)
XLA Ops:
  1.9 33.8 %shard_map.131 = (f32[1,256]{1,0:T(1,128)S(1)}, f32[1,16,256]{2,1,0:T(8,128)S(1)}) custom-call(bf16[256,1152]{1,0:T(8,128)(2,1)} %hidden_hbm.1, f32[1,16,256]{2,1,0:T(8,128)} %now_hbm.1, f32[1,16,256]{2,1,0:T(8,128)} %next_hbm.1, s32[1]{0:T(128)S(6)} %copy.18.step_hbm, s32[1]{0:T(128)S(6)} %copy.19.tag_hbm, f32[8]{0:T(128)} %level_hbm.1, ...), custom_call_target="tpu_custom_call" | custom-call | tf_op jit(solution)/shard_map/pallas_call | solution.py:437
  35.7 0.6 %copy.16 = f32[1,256]{1,0:T(1,128)} copy(f32[1,256]{1,0:T(1,128)S(1)} %get-tuple-element.2) | data formatting | bytes 2048
  36.3 0.6 %copy.17 = f32[1,16,256]{2,1,0:T(8,128)} copy(f32[1,16,256]{2,1,0:T(8,128)S(1)} %get-tuple-element.3) | data formatting | bytes 32768

commit v4 on v3

--- a/solution.py
+++ b/solution.py
@@ -195,6 +195,16 @@
 
     normed = (standard * (1.0 + entry(1)) + entry(0)).astype(bf16)
 
+    def head_norm_both(queries, keys):
+        both = jnp.concatenate([queries, keys], 0)
+        total = dot((both * both).astype(bf16), group_ref[...])
+        inverse = lax.rsqrt(total / head + norm_eps)
+        cut = queries.shape[0]
+        inverse = jnp.concatenate([inverse[:cut] * head**-0.5, inverse[cut:]], 0)
+        high, low = split_pair(inverse)
+        both = (both * dot(jnp.concatenate([high, low], 1), spread_ref[...])).astype(bf16)
+        return both[:cut], both[cut:]
+
     def head_norm(values, factor):
         total = dot((values * values).astype(bf16), group_ref[...])
         inverse = lax.rsqrt(total / head + norm_eps) * factor
@@ -218,10 +228,12 @@
         for first in range(0, HEADS, GROUP):
             group = range(first, first + GROUP)
             scores = []
-            for index in group:
+            for index in range(first, first + GROUP, 2):
                 tile, window = window_of(index)
-                own = own_lanes(index, tile)
-                scores.append(dot_t(queries[:, window] * own, k_ref[:, window]))
+                query = queries[:, window]
+                pair = [query * own_lanes(index + turn, tile) for turn in range(2)]
+                score = dot_t(jnp.concatenate(pair, 0), k_ref[:, window])
+                scores += [score[: query.shape[0]], score[query.shape[0] :]]
             weights = [jnp.exp(score).astype(bf16) for score in scores]
             if masked:
                 weights = [weight * mask_ref[...] for weight in weights]
@@ -350,8 +362,9 @@
         after = after.astype(f32).reshape(part, width)
         normed = (layer_norm(after) * (1.0 + entry(4)) + entry(3)).astype(bf16)
         after_ref[lo : lo + part, :] = after.astype(bf16)
-        q_ref[lo : lo + part, :] = head_norm(dot(normed, tqkv_w[:, 0:width]), head**-0.5)
-        k_ref[lo : lo + part, :] = head_norm(dot(normed, tqkv_w[:, width : 2 * width]), 1.0)
+        q_ref[lo : lo + part, :], k_ref[lo : lo + part, :] = head_norm_both(
+            dot(normed, tqkv_w[:, 0:width]), dot(normed, tqkv_w[:, width : 2 * width])
+        )
         v_ref[lo : lo + part, :] = dot(normed, tqkv_w[:, 2 * width :]).astype(bf16)
     attended = attend(q_ref, True)
     term = dot(attended, tout_w[...]).astype(bf16).astype(f32)

time: 37.1 us -> 36.6 us (0.987)
  Pallas kernels: 33.8 us -> 33.3 us
    pallas_call x1, Pallas kernels: 33.8 us -> 33.3 us  [shards(): pl.pallas_call(functools.partial(kernel, sizes), out_shape=(pltpu.VMEM((1...]
where the time goes in v4:
time: 36.6 us; the launch traced here: 36.4 us
  Pallas kernels  33.3 us (91%)
  between operations  1.93 us (5%)
  local copies, waits for them, and re-layouts  1.17 us (3%)
    pallas_call x1, Pallas kernels, shards(): pl.pallas_call(functools.partial(kernel, sizes), out_shape=(pltpu.VMEM((1...  33.3 us
    unnamed x2, local copies, waits for them, and re-layouts  1.17 us

profile of v4, /device:TPU:0, one launch (start us, length us, event | category | flops | bytes accessed | tf_op | source)
XLA Modules:
  0.0 36.4 jit_solution(9958019854723199339)
XLA Ops:
  1.9 33.3 %shard_map.131 = (f32[1,256]{1,0:T(1,128)S(1)}, f32[1,16,256]{2,1,0:T(8,128)S(1)}) custom-call(bf16[256,1152]{1,0:T(8,128)(2,1)} %hidden_hbm.1, f32[1,16,256]{2,1,0:T(8,128)} %now_hbm.1, f32[1,16,256]{2,1,0:T(8,128)} %next_hbm.1, s32[1]{0:T(128)S(6)} %copy.18.step_hbm, s32[1]{0:T(128)S(6)} %copy.19.tag_hbm, f32[8]{0:T(128)} %level_hbm.1, ...), custom_call_target="tpu_custom_call" | custom-call | tf_op jit(solution)/shard_map/pallas_call | solution.py:450
  35.2 0.6 %copy.16 = f32[1,256]{1,0:T(1,128)} copy(f32[1,256]{1,0:T(1,128)S(1)} %get-tuple-element.2) | data formatting | bytes 2048
  35.8 0.6 %copy.17 = f32[1,16,256]{2,1,0:T(8,128)} copy(f32[1,16,256]{2,1,0:T(8,128)S(1)} %get-tuple-element.3) | data formatting | bytes 32768

commit v5 on v4

--- a/solution.py
+++ b/solution.py
@@ -240,7 +240,7 @@
             for index, weight in zip(group, weights):
                 tile, window = window_of(index)
                 own = own_lanes(index, tile)
-                mixed = dot(weight, v_ref[:, window] * own + (1.0 - own))
+                mixed = dot(weight, jnp.where(own > 0.5, v_ref[:, window], own + 1.0))
                 for side in range(WINDOW // LANES):
                     begin = index * head - (tile + side) * LANES
                     if begin >= LANES or begin + head <= 0:
@@ -272,7 +272,7 @@
             src_ref=out_buf.at[block_of(inner_id, outer_id)],
             dst_ref=in_buf.at[my_slot],
             send_sem=send_sem.at[chunk, turn],
-            recv_sem=recv_sem.at[turn],
+            recv_sem=recv_sem.at[outer],
             device_id=(inner_id, outer_id),
             device_id_type=MESH,
         )
@@ -355,28 +355,59 @@
         load.wait()
     repeated = jnp.concatenate([final_ref[...]] * (LANES // channels), 0)
 
-    for turn in reversed(range(halves)):
-        lo = (halves - 1 - turn) * part
-        several(out_buf, in_buf, send_sem.at[0, turn], recv_sem.at[turn], partners(turn)).wait_recv()
-        after = in_buf[pl.ds(half_of(turn) * block_peers, block_peers)]
-        after = after.astype(f32).reshape(part, width)
+    stages = [[side * span + step for step in range(span)]]
+    if halves == 2:
+        for step in range(span):
+            stages.append([jnp.where(side == 0, outer_size - 1 - step, step)])
+
+    def arrive(outer_id):
+        def wait(blocks):
+            several(
+                out_buf, in_buf, send_sem.at[0, 0], recv_sem.at[outer_id], blocks
+            ).wait_recv()
+
+        pl.when(outer_id == outer)(lambda: wait(inner_size - 1))
+        pl.when(outer_id != outer)(lambda: wait(inner_size))
+
+    def enter(outer_ids, lo):
+        pieces = []
+        for outer_id in outer_ids:
+            arrive(outer_id)
+            piece = in_buf[pl.ds(outer_id * inner_size, inner_size)]
+            pieces.append(piece.astype(f32).reshape(inner_size * count, width))
+        after = jnp.concatenate(pieces, 0)
+        hi = lo + after.shape[0]
         normed = (layer_norm(after) * (1.0 + entry(4)) + entry(3)).astype(bf16)
-        after_ref[lo : lo + part, :] = after.astype(bf16)
-        q_ref[lo : lo + part, :], k_ref[lo : lo + part, :] = head_norm_both(
-            dot(normed, tqkv_w[:, 0:width]), dot(normed, tqkv_w[:, width : 2 * width])
-        )
-        v_ref[lo : lo + part, :] = dot(normed, tqkv_w[:, 2 * width :]).astype(bf16)
+        after_ref[lo:hi, :] = after.astype(bf16)
+        mixed = dot(normed, tqkv_w[:, 0 : 2 * width])
+        q_ref[lo:hi, :], k_ref[lo:hi, :] = head_norm_both(mixed[:, :width], mixed[:, width:])
+        v_ref[lo:hi, :] = dot(normed, tqkv_w[:, 2 * width :]).astype(bf16)
+
+    enter(stages[0], 0)
+    if halves == 2:
+        rim = (outer == 0) | (outer == outer_size - 1)
+        distant = [stage[0] for stage in stages[1:]]
+
+        @pl.when(rim)
+        def _():
+            enter(distant, span * inner_size * count)
+
+        @pl.when(jnp.logical_not(rim))
+        def _():
+            for step in range(span):
+                enter(distant[step : step + 1], (span + step) * inner_size * count)
+
     attended = attend(q_ref, True)
     term = dot(attended, tout_w[...]).astype(bf16).astype(f32)
     final_normed = layer_norm(after_ref[...].astype(f32) + entry(5) * term).astype(bf16)
     mixed = jnp.where(own_slot, dot_t(final_normed, repeated), 0.0)
     packed = jnp.sum(mixed.reshape(peers, count, LANES), 1)
     packed = packed.reshape(peers, 1, LANES)
-    for turn in range(halves):
-        order = halves - 1 - turn
-        back_buf[pl.ds(half_of(turn) * block_peers, block_peers)] = packed[
-            order * block_peers : (order + 1) * block_peers
-        ]
+    done = 0
+    for stage in stages:
+        blocks = len(stage) * inner_size
+        back_buf[pl.ds(stage[0] * inner_size, blocks)] = packed[done : done + blocks]
+        done += blocks
     for turn in range(halves):
 
         for step in range(span):
@@ -447,6 +478,7 @@
     exchange = pltpu.VMEM((peers, count, width), bf16)
     returned = pltpu.VMEM((peers, 1, LANES), f32)
     sems = pltpu.SemaphoreType.DMA((2,))
+    arrivals = pltpu.SemaphoreType.DMA((sizes[1],))
     return pl.pallas_call(
         functools.partial(kernel, sizes),
         out_shape=(pltpu.VMEM((1, rows), f32), pltpu.VMEM(now.shape, f32)),
@@ -479,7 +511,7 @@
             returned,
             pltpu.SemaphoreType.DMA((17,)),
             pltpu.SemaphoreType.DMA((2, 2)),
-            sems,
+            arrivals,
             sems,
             sems,
         ],

time: 36.6 us -> 36.8 us (level)
  no operation moved by 1% of the time
where the time goes in v5:
time: 36.8 us; the launch traced here: 36.6 us
  Pallas kernels  33.5 us (91%)
  between operations  1.93 us (5%)
  local copies, waits for them, and re-layouts  1.17 us (3%)
    pallas_call x1, Pallas kernels, shards(): pl.pallas_call(functools.partial(kernel, sizes), out_shape=(pltpu.VMEM((1...  33.5 us
    unnamed x2, local copies, waits for them, and re-layouts  1.17 us

profile of v5, /device:TPU:0, one launch (start us, length us, event | category | flops | bytes accessed | tf_op | source)
XLA Modules:
  0.0 36.6 jit_solution(5742402443882617735)
XLA Ops:
  1.9 33.5 %shard_map.131 = (f32[1,256]{1,0:T(1,128)S(1)}, f32[1,16,256]{2,1,0:T(8,128)S(1)}) custom-call(bf16[256,1152]{1,0:T(8,128)(2,1)} %hidden_hbm.1, f32[1,16,256]{2,1,0:T(8,128)} %now_hbm.1, f32[1,16,256]{2,1,0:T(8,128)} %next_hbm.1, s32[1]{0:T(128)S(6)} %copy.18.step_hbm, s32[1]{0:T(128)S(6)} %copy.19.tag_hbm, f32[8]{0:T(128)} %level_hbm.1, ...), custom_call_target="tpu_custom_call" | custom-call | tf_op jit(solution)/shard_map/pallas_call | solution.py:482
  35.4 0.6 %copy.16 = f32[1,256]{1,0:T(1,128)} copy(f32[1,256]{1,0:T(1,128)S(1)} %get-tuple-element.2) | data formatting | bytes 2048
  36.0 0.6 %copy.17 = f32[1,16,256]{2,1,0:T(8,128)} copy(f32[1,16,256]{2,1,0:T(8,128)S(1)} %get-tuple-element.3) | data formatting | bytes 32768

commit v6 on v5

--- a/solution.py
+++ b/solution.py
@@ -319,9 +319,9 @@
                 def _():
                     start(0)
 
-                pl.loop(1, each)(start)
+                pl.loop(1, each, unroll=True)(start)
             else:
-                pl.loop(0, each)(start)
+                pl.loop(0, each, unroll=True)(start)
 
     for chunk in range(chunks):
         lo = chunk * size
@@ -413,7 +413,7 @@
         for step in range(span):
             to_outer = half_of(turn) * span + wrap(place + step, span)
 
-            @pl.loop(1 if turn == halves - 1 and step == 0 else 0, inner_size)
+            @pl.loop(1 if turn == halves - 1 and step == 0 else 0, inner_size, unroll=True)
             def _(k):
                 backward(wrap(inner + k, inner_size), to_outer, turn).start()
 

time: 36.8 us -> 36.5 us (level)
  no operation moved by 1% of the time
where the time goes in v6:
time: 36.5 us; the launch traced here: 36.4 us
  Pallas kernels  33.3 us (91%)
  between operations  1.93 us (5%)
  local copies, waits for them, and re-layouts  1.17 us (3%)
    pallas_call x1, Pallas kernels, shards(): pl.pallas_call(functools.partial(kernel, sizes), out_shape=(pltpu.VMEM((1...  33.3 us
    unnamed x2, local copies, waits for them, and re-layouts  1.17 us

profile of v6, /device:TPU:0, one launch (start us, length us, event | category | flops | bytes accessed | tf_op | source)
XLA Modules:
  0.0 36.4 jit_solution(12663878445603256632)
XLA Ops:
  1.9 33.3 %shard_map.131 = (f32[1,256]{1,0:T(1,128)S(1)}, f32[1,16,256]{2,1,0:T(8,128)S(1)}) custom-call(bf16[256,1152]{1,0:T(8,128)(2,1)} %hidden_hbm.1, f32[1,16,256]{2,1,0:T(8,128)} %now_hbm.1, f32[1,16,256]{2,1,0:T(8,128)} %next_hbm.1, s32[1]{0:T(128)S(6)} %copy.18.step_hbm, s32[1]{0:T(128)S(6)} %copy.19.tag_hbm, f32[8]{0:T(128)} %level_hbm.1, ...), custom_call_target="tpu_custom_call" | custom-call | tf_op jit(solution)/shard_map/pallas_call | solution.py:482
  35.2 0.6 %copy.16 = f32[1,256]{1,0:T(1,128)} copy(f32[1,256]{1,0:T(1,128)S(1)} %get-tuple-element.2) | data formatting | bytes 2048
  35.8 0.6 %copy.17 = f32[1,16,256]{2,1,0:T(8,128)} copy(f32[1,16,256]{2,1,0:T(8,128)S(1)} %get-tuple-element.3) | data formatting | bytes 32768
